TPU v7x, 32 devices: a whole 2x2x4 slice. The times are simulated.
32 devices in a mesh: sweep: 2 (over x), na: 16 (over z, y, core).
Axes of the slice: x: 2, y: 2, z: 4, core: 2. Of those that a mesh axis runs over, the one named last changes fastest.
Arguments:
- hierarchy: float32 [32, 16, 2, 128, 128], P(('sweep', 'na')), parts along dimension 0, may hold values from -6 to 6
- hamiltonian: float32 [128, 128], replicated, may hold values from -0.5 to 0.5
- couplings: float32 [2, 128, 128], replicated, may hold values from -0.5 to 0.5
- damp_rates: float32 [4], P('sweep'), parts along dimension 0, may hold values from 0.5 to 2
- coef_real: float32 [4], P('sweep'), parts along dimension 0, may hold values from 0.5 to 2
- coef_imag: float32 [4], P('sweep'), parts along dimension 0, may hold values from -1 to 1
Outputs:
- evolved: float32 [32, 16, 2, 128, 128], P(('sweep', 'na')), parts along dimension 0
There are 2 independent parts, one for each index of `sweep`. A program takes and returns all parts, laid end to end along the dimension named above; an argument that names none is the same for every part. Nothing has to cross between parts.
All inputs are finite; a program needn't handle non-finite values.
Results may differ from a plain program's by a relative error of at most 0.0001.
Values sent between devices are 32-bit elements; how exact they have to be, the bound alone decides.
A program may use at most 128 MiB of HBM per device.

v0:
```python
import jax
import jax.numpy as jnp
from jax import lax
from jax.sharding import PartitionSpec as P

step_size = 0.02


def from_behind(value, axis, steps):
    count = lax.axis_size(axis)
    leading, last = (max(0, -steps), min(count, count - steps))
    return lax.ppermute(value, axis, [(source, source + steps) for source in range(leading, last)])


def swapped(value, axis, bit):
    return lax.ppermute(value, axis, [(i, i ^ 1 << bit) for i in range(lax.axis_size(axis))])


def evolve(
    values,
    raise_one,
    lower_one,
    raise_two,
    lower_two,
    first_mode,
    second_mode,
    alive_mask,
    hamilton,
    coupled,
    damp_rates,
    coef_real,
    coef_imag,
):
    matrix_order = values.shape[-1]
    magnitude = jnp.sqrt(coef_real * coef_real + coef_imag * coef_imag)
    left_terms = [values]
    right_terms = [values]
    mode_terms = ((raise_one, lower_one, first_mode), (raise_two, lower_two, second_mode))
    for which_mode in range(2):
        raised, lowered, occupied = mode_terms[which_mode]
        raise_weight = jnp.sqrt((occupied + 1.0) * magnitude[which_mode])[..., None, None]
        lower_weight = jnp.sqrt(occupied / magnitude[which_mode])[..., None, None]
        real_coef = coef_real[which_mode]
        imag_coef = coef_imag[which_mode]
        shared_re = raise_weight * raised[..., 0, :, :]
        shared_im = raise_weight * raised[..., 1, :, :]
        direct_re = lower_weight * (real_coef * lowered[..., 0, :, :])
        direct_im = lower_weight * (real_coef * lowered[..., 1, :, :])
        cross_re = lower_weight * (imag_coef * lowered[..., 1, :, :])
        cross_im = lower_weight * (imag_coef * lowered[..., 0, :, :])
        left_terms.append(
            jnp.stack([shared_re + direct_re - cross_re, shared_im + direct_im + cross_im], axis=-3)
        )
        right_terms.append(
            jnp.stack([shared_re + direct_re + cross_re, shared_im + direct_im - cross_im], axis=-3)
        )
    operators = (hamilton, coupled[0], coupled[1])
    flat_shape = (-1, 2, matrix_order, matrix_order)
    left_sum = sum(
        (
            jnp.einsum(
                "ab,scbd->scad",
                operand,
                stacked.reshape(flat_shape),
                precision=lax.Precision.HIGHEST,
            )
            for operand, stacked in zip(operators, left_terms)
        )
    )
    right_sum = sum(
        (
            jnp.einsum(
                "scab,bd->scad",
                stacked.reshape(flat_shape),
                operand,
                precision=lax.Precision.HIGHEST,
            )
            for operand, stacked in zip(operators, right_terms)
        )
    )
    damping = (first_mode * damp_rates[0] + second_mode * damp_rates[1]).reshape((-1, 1, 1))
    flat_values = values.reshape(flat_shape)
    change_re = left_sum[:, 1] - right_sum[:, 1] - damping * flat_values[:, 0]
    change_im = right_sum[:, 0] - left_sum[:, 0] - damping * flat_values[:, 1]
    change = jnp.stack([change_re, change_im], axis=1).reshape(values.shape)
    return change * alive_mask[..., None, None, None]


def neighbours(values):
    from_next = from_behind(values, "na", -1)
    from_prev = from_behind(values, "na", 1)
    return (from_next, from_prev)


def advance(values, derivative):
    middle = values + 0.5 * step_size * derivative(values)
    values = values + step_size * derivative(middle)
    return values


def per_device(hierarchy, hamiltonian, couplings, damp_rates, coef_real, coef_imag):
    hamilton = 0.5 * (hamiltonian + hamiltonian.T)
    coupled = 0.5 * (couplings + jnp.swapaxes(couplings, 1, 2))
    axis_count = lax.axis_size("na")
    position = lax.axis_index("na")
    total_slots = hierarchy.shape[1]
    slot_index = jnp.arange(total_slots)
    column_alive = (slot_index + position <= axis_count - 1)[None, :]
    values = hierarchy * column_alive.astype(jnp.float32)[..., None, None, None]
    half_slots = axis_count // 2 + 1
    bit_total = axis_count.bit_length() - 1
    spot_index = jnp.arange(half_slots)[None, :]
    lower_mask = spot_index < axis_count - position
    upper_mask = spot_index >= axis_count + 1 - position
    first_mode = jnp.where(lower_mask, position, axis_count - 1 - position).astype(jnp.float32)
    second_mode = jnp.where(lower_mask, spot_index, 2 * half_slots - 1 - spot_index).astype(
        jnp.float32
    )
    alive_mask = (lower_mask | upper_mask).astype(jnp.float32)
    lower_pick = lower_mask[..., None, None, None]
    upper_pick = upper_mask[..., None, None, None]
    shipped = jnp.concatenate(
        [jnp.zeros_like(values[:, :2]), jnp.flip(values[:, half_slots:], axis=1)], 1
    )
    for bit_index in range(bit_total):
        shipped = swapped(shipped, "na", bit_index)
    packed = values[:, :half_slots] + shipped

    def derivative(current):
        from_next, from_prev = neighbours(current)
        border = current[:, half_slots - 1 :]
        for bit_index in range(bit_total):
            border = swapped(border, "na", bit_index)
        next_spot = jnp.concatenate([current[:, 1:], border], 1)
        prev_spot = jnp.concatenate([jnp.zeros_like(current[:, :1]), current[:, :-1]], 1)
        return evolve(
            current,
            jnp.where(lower_pick, from_next, from_prev),
            jnp.where(lower_pick, from_prev, from_next),
            jnp.where(lower_pick, next_spot, prev_spot),
            jnp.where(lower_pick, prev_spot, next_spot),
            first_mode,
            second_mode,
            alive_mask,
            hamilton,
            coupled,
            damp_rates,
            coef_real,
            coef_imag,
        )

    packed = advance(packed, derivative)
    staying = jnp.where(lower_pick, packed, 0.0)
    returned = jnp.flip(jnp.where(upper_pick, packed, 0.0)[:, 2:], axis=1)
    for bit_index in range(bit_total):
        returned = swapped(returned, "na", bit_index)
    return jnp.concatenate([staying, returned], 1)


def solution(mesh):
    in_specs = (
        P(("sweep", "na"), None, None, None, None),
        P(),
        P(),
        P("sweep"),
        P("sweep"),
        P("sweep"),
    )
    out_specs = P(("sweep", "na"), None, None, None, None)
    return jax.shard_map(
        per_device, mesh=mesh, in_specs=in_specs, out_specs=out_specs, check_vma=False
    )
```

profile of v0, /device:TPU:0, one launch (start us, length us, event | category | flops | bytes accessed | tf_op | source)
XLA Modules:
  0.0 329.6 jit_solution(10514513476213963413)
XLA Ops:
  0.0 2.9 copy.7
  2.9 1.9 broadcast_multiply_fusion
  4.8 1.0 slice.211
  5.8 1.2 rev.7
  7.7 2.5 collective-permute-done
  10.2 2.9 collective-permute-start.1
  13.1 26.3 %collective-permute-done.1 = f32[1,9,2,128,128]{3,4,1,2,0:T(8,128)S(1)} collective-permute-done((f32[1,9,2,128,128]{3,4,1,2,0:T(8,128)S(1)}, f32[1,9,2,128,128]{3,4,1,2,0:T(8,128)S(1)}, u32[]{:S(2)}, u32[]{:S(2)}) %collective-permute-start.1) | collective-permute-done | bytes 1179680 | tf_op jit(solution)/shard_map/ppermute | solution.py:16
  39.4 1.8 collective-permute-start.2
  41.2 25.7 %collective-permute-done.2 = f32[1,9,2,128,128]{3,4,1,2,0:T(8,128)} collective-permute-done((f32[1,9,2,128,128]{3,4,1,2,0:T(8,128)S(1)}, f32[1,9,2,128,128]{3,4,1,2,0:T(8,128)}, u32[]{:S(2)}, u32[]{:S(2)}) %collective-permute-start.2) | collective-permute-done | bytes 1179680 | tf_op jit(solution)/shard_map/ppermute | solution.py:16
  66.9 2.5 collective-permute-start.3
  69.7 0.7 fusion.101
  70.3 0.7 fusion.102
  71.0 48.9 %collective-permute-done.3 = f32[1,9,2,128,128]{3,4,1,2,0:T(8,128)} collective-permute-done((f32[1,9,2,128,128]{3,4,1,2,0:T(8,128)}, f32[1,9,2,128,128]{3,4,1,2,0:T(8,128)}, u32[]{:S(2)}, u32[]{:S(2)}) %collective-permute-start.3) | collective-permute-done | bytes 1179680 | tf_op jit(solution)/shard_map/ppermute | solution.py:16
  120.0 1.4 slice_add_fusion
  121.4 1.4 collective-permute-start.5
  122.7 1.3 collective-permute-start.4
  124.0 1.3 multiply_add_fusion
  125.3 2.5 collective-permute-start.6
  127.9 0.7 multiply_sqrt_fusion.1
  128.5 0.7 divide_sqrt_fusion
  129.2 1.7 collective-permute-start.7
  130.9 0.6 fusion.100
  131.5 13.6 %collective-permute-done.7 = f32[1,1,2,128,128]{3,4,1,2,0:T(8,128)S(1)} collective-permute-done((f32[1,1,2,128,128]{3,4,1,2,0:T(8,128)S(1)}, f32[1,1,2,128,128]{3,4,1,2,0:T(8,128)S(1)}, u32[]{:S(2)}, u32[]{:S(2)}) %collective-permute-start.7) | collective-permute-done | bytes 131104 | tf_op jit(solution)/shard_map/ppermute | solution.py:16
  145.1 10.5 %collective-permute-start.8 = (f32[1,1,2,128,128]{3,4,1,2,0:T(8,128)S(1)}, f32[1,1,2,128,128]{3,4,1,2,0:T(8,128)S(1)}, u32[]{:S(2)}, u32[]{:S(2)}) collective-permute-start(f32[1,1,2,128,128]{3,4,1,2,0:T(8,128)S(1)} %collective-permute-done.7), channel_id=1, source_target_pairs={{0,4},{1,5},{2,6},{3,7},{4,0},{5,1},{6,2},{7,3},{8,12},{9,13},{10,... | collective-permute-start | bytes 393224 | tf_op jit(solution)/shard_map/ppermute | solution.py:16
  155.6 0.6 fusion.103
  156.2 2.3 collective-permute-done.8
  158.6 4.1 %collective-permute-start.9 = (f32[1,1,2,128,128]{3,4,1,2,0:T(8,128)S(1)}, f32[1,1,2,128,128]{3,4,1,2,0:T(8,128)S(1)}, u32[]{:S(2)}, u32[]{:S(2)}) collective-permute-start(f32[1,1,2,128,128]{3,4,1,2,0:T(8,128)S(1)} %collective-permute-done.8), channel_id=1, source_target_pairs={{0,8},{1,9},{2,10},{3,11},{4,12},{5,13},{6,14},{7,15},{8,0},{9,1},... | collective-permute-start | bytes 393224 | tf_op jit(solution)/shard_map/ppermute | solution.py:16
  162.9 4.1 %collective-permute-done.9 = f32[1,1,2,128,128]{3,4,1,2,0:T(8,128)S(1)} collective-permute-done((f32[1,1,2,128,128]{3,4,1,2,0:T(8,128)S(1)}, f32[1,1,2,128,128]{3,4,1,2,0:T(8,128)S(1)}, u32[]{:S(2)}, u32[]{:S(2)}) %collective-permute-start.9) | collective-permute-done | bytes 131104 | tf_op jit(solution)/shard_map/ppermute | solution.py:16
  167.0 2.0 broadcast_select_fusion.4
  169.0 1.7 fusion.50
  170.8 1.2 fusion.6
  172.0 1.1 fusion.30
  173.1 1.6 fusion.54
  174.7 1.2 fusion.9
  175.9 1.1 fusion.28
  177.0 1.3 fusion.3
  178.2 1.1 fusion.5
  180.0 1.4 collective-permute-start.11
  181.3 1.5 collective-permute-start.10
  182.8 2.7 collective-permute-start.12
  185.6 2.2 collective-permute-done.12
  187.8 1.1 collective-permute-start.13
  189.0 14.9 %collective-permute-done.13 = f32[1,1,2,128,128]{3,4,1,2,0:T(8,128)S(1)} collective-permute-done((f32[1,1,2,128,128]{3,4,1,2,0:T(8,128)S(1)}, f32[1,1,2,128,128]{3,4,1,2,0:T(8,128)S(1)}, u32[]{:S(2)}, u32[]{:S(2)}) %collective-permute-start.13) | collective-permute-done | bytes 131104 | tf_op jit(solution)/shard_map/ppermute | solution.py:16
  203.9 10.9 %collective-permute-start.14 = (f32[1,1,2,128,128]{3,4,1,2,0:T(8,128)S(1)}, f32[1,1,2,128,128]{3,4,1,2,0:T(8,128)S(1)}, u32[]{:S(2)}, u32[]{:S(2)}) collective-permute-start(f32[1,1,2,128,128]{3,4,1,2,0:T(8,128)S(1)} %collective-permute-done.13), channel_id=1, source_target_pairs={{0,4},{1,5},{2,6},{3,7},{4,0},{5,1},{6,2},{7,3},{8,12},{9,13},{10,... | collective-permute-start | bytes 393224 | tf_op jit(solution)/shard_map/ppermute | solution.py:16
  215.1 3.4 %collective-permute-done.14 = f32[1,1,2,128,128]{3,4,1,2,0:T(8,128)S(1)} collective-permute-done((f32[1,1,2,128,128]{3,4,1,2,0:T(8,128)S(1)}, f32[1,1,2,128,128]{3,4,1,2,0:T(8,128)S(1)}, u32[]{:S(2)}, u32[]{:S(2)}) %collective-permute-start.14) | collective-permute-done | bytes 131104 | tf_op jit(solution)/shard_map/ppermute | solution.py:16
  218.5 3.9 %collective-permute-start.15 = (f32[1,1,2,128,128]{3,4,1,2,0:T(8,128)S(1)}, f32[1,1,2,128,128]{3,4,1,2,0:T(8,128)S(1)}, u32[]{:S(2)}, u32[]{:S(2)}) collective-permute-start(f32[1,1,2,128,128]{3,4,1,2,0:T(8,128)S(1)} %collective-permute-done.14), channel_id=1, source_target_pairs={{0,8},{1,9},{2,10},{3,11},{4,12},{5,13},{6,14},{7,15},{8,0},{9,1},... | collective-permute-start | bytes 393224 | tf_op jit(solution)/shard_map/ppermute | solution.py:16
  222.6 4.1 %collective-permute-done.15 = f32[1,1,2,128,128]{3,4,1,2,0:T(8,128)S(1)} collective-permute-done((f32[1,1,2,128,128]{3,4,1,2,0:T(8,128)S(1)}, f32[1,1,2,128,128]{3,4,1,2,0:T(8,128)S(1)}, u32[]{:S(2)}, u32[]{:S(2)}) %collective-permute-start.15) | collective-permute-done | bytes 131104 | tf_op jit(solution)/shard_map/ppermute | solution.py:16
  226.7 0.8 broadcast_select_fusion.2
  227.5 1.8 fusion.58
  229.3 1.2 fusion.20
  230.5 1.1 fusion.14
  231.6 1.6 fusion.62
  233.2 1.2 fusion.23
  234.4 1.3 fusion
  235.7 1.1 fusion.17
  236.7 1.2 fusion.2
  238.3 1.3 broadcast_select_fusion
  240.0 2.5 collective-permute-done.16
  242.4 0.9 collective-permute-start.17
  243.3 21.5 %collective-permute-done.17 = f32[1,7,2,128,128]{3,4,1,2,0:T(8,128)S(1)} collective-permute-done((f32[1,7,2,128,128]{3,4,1,2,0:T(8,128)S(1)}, f32[1,7,2,128,128]{3,4,1,2,0:T(8,128)S(1)}, u32[]{:S(2)}, u32[]{:S(2)}) %collective-permute-start.17) | collective-permute-done | bytes 917536 | tf_op jit(solution)/shard_map/ppermute | solution.py:16
  265.2 21.2 %collective-permute-done.18 = f32[1,7,2,128,128]{3,4,1,2,0:T(8,128)S(1)} collective-permute-done((f32[1,7,2,128,128]{3,4,1,2,0:T(8,128)S(1)}, f32[1,7,2,128,128]{3,4,1,2,0:T(8,128)S(1)}, u32[]{:S(2)}, u32[]{:S(2)}) %collective-permute-start.18) | collective-permute-done | bytes 917536 | tf_op jit(solution)/shard_map/ppermute | solution.py:16
  286.4 2.0 collective-permute-start.19
  288.3 39.3 %collective-permute-done.19 = f32[1,7,2,128,128]{3,4,1,2,0:T(8,128)S(1)} collective-permute-done((f32[1,7,2,128,128]{3,4,1,2,0:T(8,128)S(1)}, f32[1,7,2,128,128]{3,4,1,2,0:T(8,128)S(1)}, u32[]{:S(2)}, u32[]{:S(2)}) %collective-permute-start.19) | collective-permute-done | bytes 917536 | tf_op jit(solution)/shard_map/ppermute | solution.py:16
  327.7 1.8 copy.34
  (43 shorter events, 3.4 us)
Async XLA Ops:
  7.0 62.4 %copy-start.2 = (f32[128,128]{1,0:T(8,128)S(1)}, f32[128,128]{1,0:T(8,128)}, u32[]{:S(2)}) copy-start(f32[128,128]{1,0:T(8,128)} %param.7) | copy-start | bytes 196612
  7.0 62.5 %copy-start.1 = (f32[2,128,128]{2,1,0:T(8,128)S(1)}, f32[2,128,128]{2,1,0:T(8,128)}, u32[]{:S(2)}) copy-start(f32[2,128,128]{2,1,0:T(8,128)} %param.8) | copy-start | bytes 393220
  7.0 62.6 %copy-start.4 = (f32[2]{0:T(128)S(1)}, f32[2]{0:T(128)}, u32[]{:S(2)}) copy-start(f32[2]{0:T(128)} %param.10) | copy-start | bytes 28
  7.0 62.6 %copy-start.5 = (f32[2]{0:T(128)S(1)}, f32[2]{0:T(128)}, u32[]{:S(2)}) copy-start(f32[2]{0:T(128)} %param.11) | copy-start | bytes 28
  7.1 63.3 %copy-start.3 = (f32[2]{0:T(128)S(1)}, f32[2]{0:T(128)}, u32[]{:S(2)}) copy-start(f32[2]{0:T(128)} %param.9) | copy-start | bytes 28
  7.2 3.0 collective-permute-start
  10.2 29.1 %collective-permute-start.1 = (f32[1,9,2,128,128]{3,4,1,2,0:T(8,128)S(1)}, f32[1,9,2,128,128]{3,4,1,2,0:T(8,128)S(1)}, u32[]{:S(2)}, u32[]{:S(2)}) collective-permute-start(f32[1,9,2,128,128]{3,4,1,2,0:T(8,128)S(1)} %collective-permute-done), channel_id=1, source_target_pairs={{0,2},{1,3},{2,0},{3,1},{4,6},{5,7},{6,4},{7,5},{8,10},{9,11},{10,... | collective-permute-start | bytes 3538952 | tf_op jit(solution)/shard_map/ppermute | solution.py:16
  39.4 27.5 %collective-permute-start.2 = (f32[1,9,2,128,128]{3,4,1,2,0:T(8,128)S(1)}, f32[1,9,2,128,128]{3,4,1,2,0:T(8,128)}, u32[]{:S(2)}, u32[]{:S(2)}) collective-permute-start(f32[1,9,2,128,128]{3,4,1,2,0:T(8,128)S(1)} %collective-permute-done.1), channel_id=1, source_target_pairs={{0,4},{1,5},{2,6},{3,7},{4,0},{5,1},{6,2},{7,3},{8,12},{9,13},{10,... | collective-permute-start | bytes 3538952 | tf_op jit(solution)/shard_map/ppermute | solution.py:16
  66.9 53.1 %collective-permute-start.3 = (f32[1,9,2,128,128]{3,4,1,2,0:T(8,128)}, f32[1,9,2,128,128]{3,4,1,2,0:T(8,128)}, u32[]{:S(2)}, u32[]{:S(2)}) collective-permute-start(f32[1,9,2,128,128]{3,4,1,2,0:T(8,128)} %collective-permute-done.2), channel_id=1, source_target_pairs={{0,8},{1,9},{2,10},{3,11},{4,12},{5,13},{6,14},{7,15},{8,0},{9,1},... | collective-permute-start | bytes 3538952 | tf_op jit(solution)/shard_map/ppermute | solution.py:16
  121.4 45.6 %collective-permute-start.5 = (f32[1,9,2,128,128]{3,4,1,2,0:T(8,128)S(1)}, f32[1,9,2,128,128]{3,4,1,2,0:T(8,128)S(1)}, u32[]{:S(2)}, u32[]{:S(2)}) collective-permute-start(f32[1,9,2,128,128]{3,4,1,2,0:T(8,128)S(1)} %slice_add_fusion), channel_id=1, source_target_pairs={{0,1},{1,2},{2,3},{3,4},{4,5},{5,6},{6,7},{7,8},{8,9},{9,10},{10,1... | collective-permute-start | bytes 3538952 | tf_op jit(solution)/shard_map/ppermute | solution.py:12
  122.7 44.3 %collective-permute-start.4 = (f32[1,9,2,128,128]{3,4,1,2,0:T(8,128)S(1)}, f32[1,9,2,128,128]{3,4,1,2,0:T(8,128)}, u32[]{:S(2)}, u32[]{:S(2)}) collective-permute-start(f32[1,9,2,128,128]{3,4,1,2,0:T(8,128)S(1)} %slice_add_fusion), channel_id=1, source_target_pairs={{1,0},{2,1},{3,2},{4,3},{5,4},{6,5},{7,6},{8,7},{9,8},{10,9},{11,1... | collective-permute-start | bytes 3538952 | tf_op jit(solution)/shard_map/ppermute | solution.py:12
  125.3 3.9 %collective-permute-start.6 = (f32[1,1,2,128,128]{3,4,1,2,0:T(8,128)S(1)}, f32[1,1,2,128,128]{3,4,1,2,0:T(8,128)S(1)}, u32[]{:S(2)}, u32[]{:S(2)}) collective-permute-start(f32[1,1,2,128,128]{3,4,1,2,0:T(8,128)S(1)} %slice.218), channel_id=1, source_target_pairs={{0,1},{1,0},{2,3},{3,2},{4,5},{5,4},{6,7},{7,6},{8,9},{9,8},{10,11... | collective-permute-start | bytes 393224 | tf_op jit(solution)/shard_map/ppermute | solution.py:16
  129.2 15.9 %collective-permute-start.7 = (f32[1,1,2,128,128]{3,4,1,2,0:T(8,128)S(1)}, f32[1,1,2,128,128]{3,4,1,2,0:T(8,128)S(1)}, u32[]{:S(2)}, u32[]{:S(2)}) collective-permute-start(f32[1,1,2,128,128]{3,4,1,2,0:T(8,128)S(1)} %collective-permute-done.6), channel_id=1, source_target_pairs={{0,2},{1,3},{2,0},{3,1},{4,6},{5,7},{6,4},{7,5},{8,10},{9,11},{10,... | collective-permute-start | bytes 393224 | tf_op jit(solution)/shard_map/ppermute | solution.py:16
  145.1 13.5 %collective-permute-start.8 = (f32[1,1,2,128,128]{3,4,1,2,0:T(8,128)S(1)}, f32[1,1,2,128,128]{3,4,1,2,0:T(8,128)S(1)}, u32[]{:S(2)}, u32[]{:S(2)}) collective-permute-start(f32[1,1,2,128,128]{3,4,1,2,0:T(8,128)S(1)} %collective-permute-done.7), channel_id=1, source_target_pairs={{0,4},{1,5},{2,6},{3,7},{4,0},{5,1},{6,2},{7,3},{8,12},{9,13},{10,... | collective-permute-start | bytes 393224 | tf_op jit(solution)/shard_map/ppermute | solution.py:16
  158.6 8.4 %collective-permute-start.9 = (f32[1,1,2,128,128]{3,4,1,2,0:T(8,128)S(1)}, f32[1,1,2,128,128]{3,4,1,2,0:T(8,128)S(1)}, u32[]{:S(2)}, u32[]{:S(2)}) collective-permute-start(f32[1,1,2,128,128]{3,4,1,2,0:T(8,128)S(1)} %collective-permute-done.8), channel_id=1, source_target_pairs={{0,8},{1,9},{2,10},{3,11},{4,12},{5,13},{6,14},{7,15},{8,0},{9,1},... | collective-permute-start | bytes 393224 | tf_op jit(solution)/shard_map/ppermute | solution.py:16
  180.0 46.8 %collective-permute-start.11 = (f32[1,9,2,128,128]{3,4,1,2,0:T(8,128)S(1)}, f32[1,9,2,128,128]{3,4,1,2,0:T(8,128)S(1)}, u32[]{:S(2)}, u32[]{:S(2)}) collective-permute-start(f32[1,9,2,128,128]{3,4,1,2,0:T(8,128)S(1)} %fusion.13), channel_id=1, source_target_pairs={{0,1},{1,2},{2,3},{3,4},{4,5},{5,6},{6,7},{7,8},{8,9},{9,10},{10,1... | collective-permute-start | bytes 3538952 | tf_op jit(solution)/shard_map/ppermute | solution.py:12
  181.3 45.4 %collective-permute-start.10 = (f32[1,9,2,128,128]{3,4,1,2,0:T(8,128)S(1)}, f32[1,9,2,128,128]{3,4,1,2,0:T(8,128)S(1)}, u32[]{:S(2)}, u32[]{:S(2)}) collective-permute-start(f32[1,9,2,128,128]{3,4,1,2,0:T(8,128)S(1)} %fusion.13), channel_id=1, source_target_pairs={{1,0},{2,1},{3,2},{4,3},{5,4},{6,5},{7,6},{8,7},{9,8},{10,9},{11,1... | collective-permute-start | bytes 3538952 | tf_op jit(solution)/shard_map/ppermute | solution.py:12
  182.8 5.0 %collective-permute-start.12 = (f32[1,1,2,128,128]{3,4,1,2,0:T(8,128)S(1)}, f32[1,1,2,128,128]{3,4,1,2,0:T(8,128)S(1)}, u32[]{:S(2)}, u32[]{:S(2)}) collective-permute-start(f32[1,1,2,128,128]{3,4,1,2,0:T(8,128)S(1)} %slice.236), channel_id=1, source_target_pairs={{0,1},{1,0},{2,3},{3,2},{4,5},{5,4},{6,7},{7,6},{8,9},{9,8},{10,11... | collective-permute-start | bytes 393224 | tf_op jit(solution)/shard_map/ppermute | solution.py:16
  187.8 16.1 %collective-permute-start.13 = (f32[1,1,2,128,128]{3,4,1,2,0:T(8,128)S(1)}, f32[1,1,2,128,128]{3,4,1,2,0:T(8,128)S(1)}, u32[]{:S(2)}, u32[]{:S(2)}) collective-permute-start(f32[1,1,2,128,128]{3,4,1,2,0:T(8,128)S(1)} %collective-permute-done.12), channel_id=1, source_target_pairs={{0,2},{1,3},{2,0},{3,1},{4,6},{5,7},{6,4},{7,5},{8,10},{9,11},{10,... | collective-permute-start | bytes 393224 | tf_op jit(solution)/shard_map/ppermute | solution.py:16
  203.9 14.6 %collective-permute-start.14 = (f32[1,1,2,128,128]{3,4,1,2,0:T(8,128)S(1)}, f32[1,1,2,128,128]{3,4,1,2,0:T(8,128)S(1)}, u32[]{:S(2)}, u32[]{:S(2)}) collective-permute-start(f32[1,1,2,128,128]{3,4,1,2,0:T(8,128)S(1)} %collective-permute-done.13), channel_id=1, source_target_pairs={{0,4},{1,5},{2,6},{3,7},{4,0},{5,1},{6,2},{7,3},{8,12},{9,13},{10,... | collective-permute-start | bytes 393224 | tf_op jit(solution)/shard_map/ppermute | solution.py:16
  218.5 8.2 %collective-permute-start.15 = (f32[1,1,2,128,128]{3,4,1,2,0:T(8,128)S(1)}, f32[1,1,2,128,128]{3,4,1,2,0:T(8,128)S(1)}, u32[]{:S(2)}, u32[]{:S(2)}) collective-permute-start(f32[1,1,2,128,128]{3,4,1,2,0:T(8,128)S(1)} %collective-permute-done.14), channel_id=1, source_target_pairs={{0,8},{1,9},{2,10},{3,11},{4,12},{5,13},{6,14},{7,15},{8,0},{9,1},... | collective-permute-start | bytes 393224 | tf_op jit(solution)/shard_map/ppermute | solution.py:16
  239.8 87.8 %copy-start = (f32[1,9,2,128,128]{3,4,1,2,0:T(8,128)S(1)}, f32[1,9,2,128,128]{3,4,1,2,0:T(8,128)}, u32[]{:S(2)}) copy-start(f32[1,9,2,128,128]{3,4,1,2,0:T(8,128)} %get-tuple-element.5) | copy-start | bytes 3538948
  239.9 2.5 collective-permute-start.16
  242.4 22.4 %collective-permute-start.17 = (f32[1,7,2,128,128]{3,4,1,2,0:T(8,128)S(1)}, f32[1,7,2,128,128]{3,4,1,2,0:T(8,128)S(1)}, u32[]{:S(2)}, u32[]{:S(2)}) collective-permute-start(f32[1,7,2,128,128]{3,4,1,2,0:T(8,128)S(1)} %collective-permute-done.16), channel_id=1, source_target_pairs={{0,2},{1,3},{2,0},{3,1},{4,6},{5,7},{6,4},{7,5},{8,10},{9,11},{10,... | collective-permute-start | bytes 2752520 | tf_op jit(solution)/shard_map/ppermute | solution.py:16
  264.8 21.5 %collective-permute-start.18 = (f32[1,7,2,128,128]{3,4,1,2,0:T(8,128)S(1)}, f32[1,7,2,128,128]{3,4,1,2,0:T(8,128)S(1)}, u32[]{:S(2)}, u32[]{:S(2)}) collective-permute-start(f32[1,7,2,128,128]{3,4,1,2,0:T(8,128)S(1)} %collective-permute-done.17), channel_id=1, source_target_pairs={{0,4},{1,5},{2,6},{3,7},{4,0},{5,1},{6,2},{7,3},{8,12},{9,13},{10,... | collective-permute-start | bytes 2752520 | tf_op jit(solution)/shard_map/ppermute | solution.py:16
  286.4 41.2 %collective-permute-start.19 = (f32[1,7,2,128,128]{3,4,1,2,0:T(8,128)S(1)}, f32[1,7,2,128,128]{3,4,1,2,0:T(8,128)S(1)}, u32[]{:S(2)}, u32[]{:S(2)}) collective-permute-start(f32[1,7,2,128,128]{3,4,1,2,0:T(8,128)S(1)} %collective-permute-done.18), channel_id=1, source_target_pairs={{0,8},{1,9},{2,10},{3,11},{4,12},{5,13},{6,14},{7,15},{8,0},{9,1},... | collective-permute-start | bytes 2752520 | tf_op jit(solution)/shard_map/ppermute | solution.py:16
where the time goes:
time: 330 us
  waiting for transfers between devices  233 us (71%)
  starting transfers between devices  54 us (16%)
  other arithmetic  18.2 us (6%)
  matrix products  14 us (4%)
  local copies, waits for them, and re-layouts  10.4 us (3%)
    ppermute x16, waiting for transfers between devices, swapped(): lax.ppermute(value, axis, [(i, i ^ 1 << bit) for i in range(lax.axis_size...  233 us
    ppermute x16, starting transfers between devices, swapped(): lax.ppermute(value, axis, [(i, i ^ 1 << bit) for i in range(lax.axis_size...  48.5 us
    dot_general x6, matrix products, evolve(): jnp.einsum('scab,bd->scad', stacked.reshape(flat_shape), operand, precisi...  7.26 us
    dot_general x6, matrix products, evolve(): jnp.einsum('ab,scbd->scad', operand, stacked.reshape(flat_shape), precisi...  6.76 us
    add x4, other arithmetic, evolve(): shared_re + direct_re + cross_re  6.67 us
  transfers between devices with their start and end apart: 20, of which 15 were waited for; matrix products, arithmetic and copies ran while one was open for 2% of the time, Pallas kernels for 0%

commit v1 on v0

v1 whole, which is shorter than its diff:
```python
import functools
import jax
import jax.numpy as jnp
from jax import lax
from jax.experimental import pallas as pl
from jax.experimental.pallas import tpu as pltpu
from jax.sharding import PartitionSpec as P

step_size = 0.02
MESH = pl.DeviceIdType.MESH
NEAR, OWN, PARTNER, FAR = 0, 1, 2, 3
STRIP = 32


def split(x):
    high = x.astype(jnp.bfloat16)
    return high, (x - high.astype(jnp.float32)).astype(jnp.bfloat16)


def kernel(
    total,
    order,
    hier_ref,
    ham_ref,
    coup_ref,
    damp_ref,
    creal_ref,
    cimag_ref,
    out_ref,
    rho,
    mid,
    w_left,
    w_right,
    x_left,
    x_right,
    table,
    own_sem,
    send_sem,
    recv_sem,
):
    M, N = order, total
    p = lax.axis_index("na")
    chip = p // 2
    core = p % 2
    odd = chip % 2
    chips = N // 2
    first = core == 0
    K = N - p
    pairs = N - 1 - 2 * chip

    is_relay = core != odd
    relays = jnp.logical_and(
        is_relay, jnp.where(odd == 1, chip >= 2, chip + 2 < chips)
    )
    fed_by_relay = jnp.logical_and(
        core == odd, jnp.where(odd == 1, chip + 2 < chips, chip >= 2)
    )
    direct_to = jnp.where(odd == 1, 2 * chip - 1, 2 * chip + 2)
    relay_to = jnp.where(odd == 1, p - 3, p + 3)
    relay_from = jnp.where(odd == 1, p + 3, p - 3)

    direct_count = jnp.where(p == 0, K - 2, K)
    near_count = jnp.where(first, jnp.where(p == 0, 0, K + 1), K - 1)
    far_count = jnp.where(
        first,
        jnp.where(
            p == 0, 0, jnp.where(jnp.logical_and(odd == 1, chip >= 2), K + 2, K)
        ),
        jnp.maximum(K - 2, 0),
    )
    relay_near_count = jnp.where(relays, jnp.where(first, near_count, K - 3), 0)
    relay_far_count = jnp.where(relays, far_count, 0)
    mid_near_count = jnp.where(first, jnp.where(p == 0, 0, K), K - 1)
    direct_slot = jnp.where(core == odd, FAR, NEAR)

    def own_copy(i):
        return pltpu.make_async_copy(
            hier_ref.at[0, i], rho.at[OWN, i], own_sem.at[i]
        )

    def remote(src, dst, send, recv, i, target):
        return pltpu.make_async_remote_copy(
            src_ref=src,
            dst_ref=dst,
            send_sem=send_sem.at[send, i],
            recv_sem=recv_sem.at[recv, i],
            device_id={"na": target},
            device_id_type=MESH,
        )

    def direct_copy(i):
        return remote(
            hier_ref.at[0, i], rho.at[direct_slot, i], 0, direct_slot, i, direct_to
        )

    def partner_copy(i):
        return remote(
            hier_ref.at[0, i], rho.at[PARTNER, i], 1, PARTNER, i, p + 1 - 2 * core
        )

    def relay_near(i):
        return remote(rho.at[NEAR, i], rho.at[FAR, i], 2, FAR, i, relay_to)

    def relay_far(i):
        return remote(rho.at[FAR, i], rho.at[NEAR, i], 3, NEAR, i, relay_to)

    def mid_copy(i):
        return remote(
            mid.at[OWN, i], mid.at[PARTNER, i], 4, 1, i, p + 1 - 2 * core
        )

    def arrival(which, i):
        return remote(
            rho.at[which, i], rho.at[which, i], 0, which, i, p + 1 - 2 * core
        )

    @pl.loop(0, K)
    def _(i):
        own_copy(i).start()

    barrier = pltpu.get_barrier_semaphore()

    def greet(target):
        pl.semaphore_signal(
            barrier, inc=1, device_id={"na": target}, device_id_type=MESH
        )

    greet(p + 1 - 2 * core)
    greet(direct_to)

    @pl.when(is_relay)
    def _():
        greet(jnp.where(odd == 1, p - 2, p + 2))

    @pl.when(relays)
    def _():
        greet(relay_to)

    @pl.when(fed_by_relay)
    def _():
        greet(relay_from)

    pl.semaphore_wait(
        barrier,
        2
        + is_relay.astype(jnp.int32)
        + relays.astype(jnp.int32)
        + fed_by_relay.astype(jnp.int32),
    )

    @pl.loop(0, K)
    def _(i):
        @pl.when(i < direct_count)
        def _():
            direct_copy(i).start()

        @pl.when(i < pairs)
        def _():
            partner_copy(i).start()

    for k in range(3):
        raw = ham_ref[...] if k == 0 else coup_ref[k - 1]
        high, low = split(0.5 * (raw + raw.T))
        for half in range(2):
            cols = slice((3 * half + k) * M, (3 * half + k + 1) * M)
            w_left[0:M, cols] = high
            w_left[M : 2 * M, cols] = low
            w_right[cols, 0:M] = high
            w_right[cols, M : 2 * M] = low

    for mode in range(2):
        re = jnp.full((8, M), creal_ref[mode], jnp.float32)
        im = jnp.full((8, M), cimag_ref[mode], jnp.float32)
        magnitude = jnp.sqrt(re * re + im * im)

        @pl.loop(0, N)
        def _(n):
            occupied = jnp.full((8, M), n.astype(jnp.float32), jnp.float32)
            lower = jnp.sqrt(occupied / magnitude)
            table[3 * mode, n] = jnp.sqrt((occupied + 1.0) * magnitude)
            table[3 * mode + 1, n] = lower * re
            table[3 * mode + 2, n] = lower * im

    @pl.loop(K, N)
    def _(i):
        out_ref[0, i] = jnp.zeros((2, M, M), jnp.float32)

    def derivative(buf, own, up, down, q, n, base, scale, store):
        alive = q + n < N - 1
        alive_scale = jnp.where(alive, 1.0, 0.0)
        up = jnp.where(alive, up, own)
        above = jnp.where(alive, n + 1, n)
        below = jnp.maximum(n - 1, 0)
        terms = []
        for mode, occupied in ((0, q), (1, n)):
            terms.append(
                (
                    table[3 * mode, occupied, 0:1, :] * alive_scale,
                    table[3 * mode + 1, occupied, 0:1, :],
                    table[3 * mode + 2, occupied, 0:1, :],
                )
            )
        sources = (((up, n), (down, n)), ((own, above), (own, below)))

        def put(block, rows, part, left, right):
            for x, is_left in ((left, True), (right, False)):
                high, low = split(x)
                for half, value in ((0, high), (1, low)):
                    at = (3 * half + block) * M
                    if is_left:
                        x_left[
                            at + rows : at + rows + STRIP, part * M : (part + 1) * M
                        ] = value
                    else:
                        x_right[
                            part * M + rows : part * M + rows + STRIP, at : at + M
                        ] = value

        for rows in range(0, M, STRIP):
            strip = slice(rows, rows + STRIP)
            for part in range(2):
                high, low = split(buf[own, n, part, strip, :])
                for half, value in ((0, high), (1, low)):
                    at = 3 * half * M
                    x_left[
                        at + rows : at + rows + STRIP, part * M : (part + 1) * M
                    ] = value
                    x_right[
                        part * M + rows : part * M + rows + STRIP, at : at + M
                    ] = value
            for mode in range(2):
                raise_w, direct_w, cross_w = terms[mode]
                (ub, us), (vb, vs) = sources[mode]
                v_re = buf[vb, vs, 0, strip, :]
                v_im = buf[vb, vs, 1, strip, :]
                e_re = raise_w * buf[ub, us, 0, strip, :] + direct_w * v_re
                e_im = raise_w * buf[ub, us, 1, strip, :] + direct_w * v_im
                x_re = cross_w * v_im
                x_im = cross_w * v_re
                put(1 + mode, rows, 0, e_re - x_re, e_re + x_re)
                put(1 + mode, rows, 1, e_im + x_im, e_im - x_im)
        left = jnp.dot(w_left[...], x_left[...], preferred_element_type=jnp.float32)
        right = jnp.dot(x_right[...], w_right[...], preferred_element_type=jnp.float32)
        damping = q.astype(jnp.float32) * damp_ref[0] + n.astype(jnp.float32) * damp_ref[1]
        left = left[0:M] + left[M : 2 * M]
        right = right[:, 0:M] + right[:, M : 2 * M]
        change_re = left[:, M : 2 * M] - right[M : 2 * M] - damping * buf[own, n, 0]
        change_im = right[0:M] - left[:, 0:M] - damping * buf[own, n, 1]
        store(0, base(0) + scale * change_re)
        store(1, base(1) + scale * change_im)

    up = jnp.where(first, PARTNER, NEAR)
    down = jnp.where(first, jnp.where(p == 0, OWN, NEAR), PARTNER)
    near_up = jnp.where(first, OWN, FAR)
    near_down = jnp.where(first, FAR, OWN)
    near_q = jnp.where(first, p - 1, p + 1)

    def take(i):
        @pl.when(i < K)
        def _():
            own_copy(i).wait()

        @pl.when(i < near_count)
        def _():
            arrival(NEAR, i).wait_recv()

        @pl.when(i < relay_near_count)
        def _():
            relay_near(i).start()

        @pl.when(i < far_count)
        def _():
            arrival(FAR, i).wait_recv()

        @pl.when(i < relay_far_count)
        def _():
            relay_far(i).start()

    take(jnp.int32(0))

    @pl.loop(0, K + 2)
    def _(i):
        take(i + 1)

        @pl.when(i < pairs)
        def _():
            arrival(PARTNER, i).wait_recv()

        @pl.when(i < K)
        def _():
            def store(part, value):
                mid[OWN, i, part] = value

            derivative(
                rho, OWN, up, down, p, i,
                lambda part: rho[OWN, i, part], 0.5 * step_size, store,
            )

        @pl.when(i < mid_near_count)
        def _():
            def store(part, value):
                mid[NEAR, i, part] = value

            derivative(
                rho, NEAR, near_up, near_down, near_q, i,
                lambda part: rho[NEAR, i, part], 0.5 * step_size, store,
            )

        @pl.when(i < pairs)
        def _():
            mid_copy(i).start()

        @pl.when(i >= 2)
        def _():
            j = i - 2

            @pl.when(j < pairs)
            def _():
                mid_copy(j).wait_recv()

            def store(part, value):
                out_ref[0, j, part] = value

            derivative(
                mid, OWN, up, down, p, j,
                lambda part: rho[OWN, j, part], step_size, store,
            )

    @pl.loop(0, N)
    def _(i):
        @pl.when(i < direct_count)
        def _():
            direct_copy(i).wait_send()

        @pl.when(i < pairs)
        def _():
            partner_copy(i).wait_send()
            mid_copy(i).wait_send()

        @pl.when(i < relay_near_count)
        def _():
            relay_near(i).wait_send()

        @pl.when(i < relay_far_count)
        def _():
            relay_far(i).wait_send()


def per_device(hierarchy, hamiltonian, couplings, damp_rates, coef_real, coef_imag):
    total = hierarchy.shape[1]
    M = hierarchy.shape[-1]
    vmem = pl.BlockSpec(memory_space=pltpu.VMEM)
    smem = pl.BlockSpec(memory_space=pltpu.SMEM)
    return pl.pallas_call(
        functools.partial(kernel, total, M),
        out_shape=jax.ShapeDtypeStruct(hierarchy.shape, jnp.float32),
        in_specs=[pl.BlockSpec(memory_space=pl.ANY), vmem, vmem, smem, smem, smem],
        out_specs=vmem,
        scratch_shapes=[
            pltpu.VMEM((4, total, 2, M, M), jnp.float32),
            pltpu.VMEM((3, total, 2, M, M), jnp.float32),
            pltpu.VMEM((2 * M, 6 * M), jnp.bfloat16),
            pltpu.VMEM((6 * M, 2 * M), jnp.bfloat16),
            pltpu.VMEM((6 * M, 2 * M), jnp.bfloat16),
            pltpu.VMEM((2 * M, 6 * M), jnp.bfloat16),
            pltpu.VMEM((6, total, 8, M), jnp.float32),
            pltpu.SemaphoreType.DMA((total,)),
            pltpu.SemaphoreType.DMA((5, total)),
            pltpu.SemaphoreType.DMA((4, total)),
        ],
        compiler_params=pltpu.CompilerParams(
            collective_id=0, has_side_effects=True, vmem_limit_bytes=60 * 2**20
        ),
    )(hierarchy, hamiltonian, couplings, damp_rates, coef_real, coef_imag)


def solution(mesh):
    in_specs = (
        P(("sweep", "na"), None, None, None, None),
        P(),
        P(),
        P("sweep"),
        P("sweep"),
        P("sweep"),
    )
    out_specs = P(("sweep", "na"), None, None, None, None)
    return jax.shard_map(
        per_device, mesh=mesh, in_specs=in_specs, out_specs=out_specs, check_vma=False
    )
```

time: 330 us -> 55.9 us (0.17)
  waiting for transfers between devices: 233 us -> 0 us
  starting transfers between devices: 54 us -> 0 us
  Pallas kernels: 0 us -> 52.6 us
  other arithmetic: 18.2 us -> 0 us
  matrix products: 14 us -> 0 us
  local copies, waits for them, and re-layouts: 10.4 us -> 3.14 us
    ppermute x20 -> x0, waiting for transfers between devices: 233 us -> none  [the longest x16 233 us: swapped(): lax.ppermute(value, axis, [(i, i ^ 1 << bit) for i in range(lax.axis_size...]
    ppermute x20 -> x0, starting transfers between devices: 54 us -> none  [the longest x16 48.5 us: swapped(): lax.ppermute(value, axis, [(i, i ^ 1 << bit) for i in range(lax.axis_size...]
    pallas_call x0 -> x1, Pallas kernels: none -> 52.6 us  [per_device(): pl.pallas_call(functools.partial(kernel, total, M), out_shape=jax.ShapeDt...]
    dot_general x12 -> x0, matrix products: 14 us -> none  [the longest x6 7.26 us: evolve(): jnp.einsum('scab,bd->scad', stacked.reshape(flat_shape), operand, precisi...]
    add x7 -> x0, other arithmetic: 9.59 us -> none  [the longest x4 6.67 us: evolve(): shared_re + direct_re + cross_re]
    select_n x4 -> x0, other arithmetic: 4.26 us -> none  [the longest x2 2.79 us: derivative(): jnp.where(lower_pick, from_next, from_prev)]
    slice x10 -> x0, local copies, waits for them, and re-layouts: 4.08 us -> none  [the longest x1 0.99 us: per_device(): values[:, half_slots:]]
  transfers between devices with their start and end apart: 20 -> 0, of which waited for: 15 -> 0; matrix products, arithmetic and copies ran while one was open for 2% -> 0% of each run, Pallas kernels for 0% -> 0%
where the time goes in v1:
time: 55.9 us; the launch traced here: 55.8 us
  Pallas kernels  52.6 us (94%)
  local copies, waits for them, and re-layouts  3.14 us (6%)
    pallas_call x1, Pallas kernels, per_device(): pl.pallas_call(functools.partial(kernel, total, M), out_shape=jax.ShapeDt...  52.6 us
    unnamed x1, local copies, waits for them, and re-layouts  3.14 us

profile of v1, /device:TPU:0, one launch (start us, length us, event | category | flops | bytes accessed | tf_op | source)
XLA Modules:
  0.0 55.8 jit_solution(15234682775526162556)
XLA Ops:
  0.0 52.6 %shard_map.64 = f32[1,16,2,128,128]{4,3,2,1,0:T(8,128)} custom-call(f32[1,16,2,128,128]{4,3,2,1,0:T(8,128)} %hier_ref.1, f32[128,128]{1,0:T(8,128)} %ham_ref.1, f32[2,128,128]{2,1,0:T(8,128)} %coup_ref.1, f32[2]{0:T(128)} %damp_ref.1, f32[2]{0:T(128)} %creal_ref.1, f32[2]{0:T(128)} %cimag_ref.1), custom_call_target="tpu_custom_call" | custom-call | tf_op jit(solution)/shard_map/pallas_call | solution.py:354
  52.6 3.1 %copy.8 = f32[1,16,2,128,128]{4,3,2,1,0:T(8,128)} copy(f32[1,16,2,128,128]{4,3,2,1,0:T(8,128)} %shard_map.64) | data formatting | bytes 4194304

commit v2 on v1

--- a/solution.py
+++ b/solution.py
@@ -34,7 +34,11 @@
     x_left,
     x_right,
     table,
+    out_buf,
+    ham_buf,
     own_sem,
+    out_sem,
+    ham_sem,
     send_sem,
     recv_sem,
 ):
@@ -78,6 +82,14 @@
             hier_ref.at[0, i], rho.at[OWN, i], own_sem.at[i]
         )
 
+    def operator_copy(k):
+        return pltpu.make_async_copy(
+            ham_ref if k == 0 else coup_ref.at[k - 1], ham_buf.at[k], ham_sem.at[k]
+        )
+
+    def out_copy(i):
+        return pltpu.make_async_copy(out_buf.at[i], out_ref.at[0, i], out_sem.at[i])
+
     def remote(src, dst, send, recv, i, target):
         return pltpu.make_async_remote_copy(
             src_ref=src,
@@ -114,10 +126,6 @@
             rho.at[which, i], rho.at[which, i], 0, which, i, p + 1 - 2 * core
         )
 
-    @pl.loop(0, K)
-    def _(i):
-        own_copy(i).start()
-
     barrier = pltpu.get_barrier_semaphore()
 
     def greet(target):
@@ -159,7 +167,15 @@
             partner_copy(i).start()
 
     for k in range(3):
-        raw = ham_ref[...] if k == 0 else coup_ref[k - 1]
+        operator_copy(k).start()
+
+    @pl.loop(0, K)
+    def _(i):
+        own_copy(i).start()
+
+    for k in range(3):
+        operator_copy(k).wait()
+        raw = ham_buf[k]
         high, low = split(0.5 * (raw + raw.T))
         for half in range(2):
             cols = slice((3 * half + k) * M, (3 * half + k + 1) * M)
@@ -183,7 +199,7 @@
 
     @pl.loop(K, N)
     def _(i):
-        out_ref[0, i] = jnp.zeros((2, M, M), jnp.float32)
+        out_buf[i] = jnp.zeros((2, M, M), jnp.float32)
 
     def derivative(buf, own, up, down, q, n, base, scale, store):
         alive = q + n < N - 1
@@ -255,11 +271,12 @@
     near_down = jnp.where(first, FAR, OWN)
     near_q = jnp.where(first, p - 1, p + 1)
 
+    def take_own(i):
+        @pl.when(i < K)
+        def _():
+            own_copy(i).wait()
+
     def take(i):
-        @pl.when(i < K)
-        def _():
-            own_copy(i).wait()
-
         @pl.when(i < near_count)
         def _():
             arrival(NEAR, i).wait_recv()
@@ -276,55 +293,63 @@
         def _():
             relay_far(i).start()
 
-    take(jnp.int32(0))
-
-    @pl.loop(0, K + 2)
-    def _(i):
+    def middle(which, i, up, down, q):
+        def store(part, value):
+            mid[which, i, part] = value
+
+        derivative(
+            rho, which, up, down, q, i,
+            lambda part: rho[which, i, part], 0.5 * step_size, store,
+        )
+
+    take_own(jnp.int32(0))
+
+    @pl.loop(K, N)
+    def _(i):
+        out_copy(i).start()
+
+    @pl.loop(-1, K)
+    def _(i):
+        take_own(i + 2)
         take(i + 1)
 
-        @pl.when(i < pairs)
-        def _():
-            arrival(PARTNER, i).wait_recv()
-
-        @pl.when(i < K)
-        def _():
+        @pl.when(i + 1 < pairs)
+        def _():
+            arrival(PARTNER, i + 1).wait_recv()
+
+        @pl.when(i + 1 < K)
+        def _():
+            middle(OWN, i + 1, up, down, p)
+
+        @pl.when(jnp.logical_and(i >= 0, i < mid_near_count))
+        def _():
+            middle(NEAR, i, near_up, near_down, near_q)
+
+        @pl.when(i + 1 < pairs)
+        def _():
+            mid_copy(i + 1).start()
+
+        @pl.when(i >= 1)
+        def _():
+            out_copy(i - 1).start()
+
+        @pl.when(i >= 0)
+        def _():
+            @pl.when(i < pairs)
+            def _():
+                mid_copy(i).wait_recv()
+
             def store(part, value):
-                mid[OWN, i, part] = value
+                out_buf[i, part] = value
 
             derivative(
-                rho, OWN, up, down, p, i,
-                lambda part: rho[OWN, i, part], 0.5 * step_size, store,
+                mid, OWN, up, down, p, i,
+                lambda part: rho[OWN, i, part], step_size, store,
             )
 
-        @pl.when(i < mid_near_count)
-        def _():
-            def store(part, value):
-                mid[NEAR, i, part] = value
-
-            derivative(
-                rho, NEAR, near_up, near_down, near_q, i,
-                lambda part: rho[NEAR, i, part], 0.5 * step_size, store,
-            )
-
-        @pl.when(i < pairs)
-        def _():
-            mid_copy(i).start()
-
-        @pl.when(i >= 2)
-        def _():
-            j = i - 2
-
-            @pl.when(j < pairs)
-            def _():
-                mid_copy(j).wait_recv()
-
-            def store(part, value):
-                out_ref[0, j, part] = value
-
-            derivative(
-                mid, OWN, up, down, p, j,
-                lambda part: rho[OWN, j, part], step_size, store,
-            )
+    take(K + 1)
+
+    out_copy(K - 1).start()
 
     @pl.loop(0, N)
     def _(i):
@@ -344,18 +369,20 @@
         @pl.when(i < relay_far_count)
         def _():
             relay_far(i).wait_send()
+
+        out_copy(i).wait()
 
 
 def per_device(hierarchy, hamiltonian, couplings, damp_rates, coef_real, coef_imag):
     total = hierarchy.shape[1]
     M = hierarchy.shape[-1]
-    vmem = pl.BlockSpec(memory_space=pltpu.VMEM)
+    hbm = pl.BlockSpec(memory_space=pltpu.HBM)
     smem = pl.BlockSpec(memory_space=pltpu.SMEM)
     return pl.pallas_call(
         functools.partial(kernel, total, M),
         out_shape=jax.ShapeDtypeStruct(hierarchy.shape, jnp.float32),
-        in_specs=[pl.BlockSpec(memory_space=pl.ANY), vmem, vmem, smem, smem, smem],
-        out_specs=vmem,
+        in_specs=[hbm] * 3 + [smem] * 3,
+        out_specs=pl.BlockSpec(memory_space=pl.ANY),
         scratch_shapes=[
             pltpu.VMEM((4, total, 2, M, M), jnp.float32),
             pltpu.VMEM((3, total, 2, M, M), jnp.float32),
@@ -364,12 +391,16 @@
             pltpu.VMEM((6 * M, 2 * M), jnp.bfloat16),
             pltpu.VMEM((2 * M, 6 * M), jnp.bfloat16),
             pltpu.VMEM((6, total, 8, M), jnp.float32),
+            pltpu.VMEM((total, 2, M, M), jnp.float32),
+            pltpu.VMEM((3, M, M), jnp.float32),
             pltpu.SemaphoreType.DMA((total,)),
+            pltpu.SemaphoreType.DMA((total,)),
+            pltpu.SemaphoreType.DMA((3,)),
             pltpu.SemaphoreType.DMA((5, total)),
             pltpu.SemaphoreType.DMA((4, total)),
         ],
         compiler_params=pltpu.CompilerParams(
-            collective_id=0, has_side_effects=True, vmem_limit_bytes=60 * 2**20
+            collective_id=0, has_side_effects=True, vmem_limit_bytes=(8 + total) * 2**20
         ),
     )(hierarchy, hamiltonian, couplings, damp_rates, coef_real, coef_imag)
 

time: 55.9 us -> 60.2 us (1.077)
  the two profiles are of different devices: /device:TPU:0 before, /device:TPU:4 now
where the time goes in v2:
time: 60.2 us; the launch traced here: 60 us
  Pallas kernels  53.4 us (89%)
  local copies, waits for them, and re-layouts  6.62 us (11%)
    pallas_call x1, Pallas kernels, per_device(): pl.pallas_call(functools.partial(kernel, total, M), out_shape=jax.ShapeDt...  53.4 us
    unnamed x13, local copies, waits for them, and re-layouts  6.62 us

profile of v2, /device:TPU:4, one launch (start us, length us, event | category | flops | bytes accessed | tf_op | source)
XLA Modules:
  0.0 60.0 jit_solution(10300089503934822358)
XLA Ops:
  0.0 0.0 copy-start
  0.0 1.6 %copy-done = f32[1,16,2,128,128]{4,3,2,1,0:T(8,128)S(1)} copy-done((f32[1,16,2,128,128]{4,3,2,1,0:T(8,128)S(1)}, f32[1,16,2,128,128]{4,3,2,1,0:T(8,128)}, u32[]{:S(2)}) %copy-start) | copy-done | bytes 2097176
  1.6 0.0 copy-start.1
  1.6 0.9 %copy-done.1 = f32[2,128,128]{2,1,0:T(8,128)S(1)} copy-done((f32[2,128,128]{2,1,0:T(8,128)S(1)}, f32[2,128,128]{2,1,0:T(8,128)}, u32[]{:S(2)}) %copy-start.1) | copy-done | bytes 131096
  2.5 0.0 copy-start.2
  2.5 0.8 %copy-done.2 = f32[128,128]{1,0:T(8,128)S(1)} copy-done((f32[128,128]{1,0:T(8,128)S(1)}, f32[128,128]{1,0:T(8,128)}, u32[]{:S(2)}) %copy-start.2) | copy-done | bytes 65560
  3.3 0.0 copy-start.3
  3.3 0.7 %copy-done.3 = f32[2]{0:T(128)S(1)} copy-done((f32[2]{0:T(128)S(1)}, f32[2]{0:T(128)}, u32[]{:S(2)}) %copy-start.3) | copy-done | bytes 32
  4.0 0.0 copy-start.4
  4.0 0.7 %copy-done.4 = f32[2]{0:T(128)S(1)} copy-done((f32[2]{0:T(128)S(1)}, f32[2]{0:T(128)}, u32[]{:S(2)}) %copy-start.4) | copy-done | bytes 32
  4.6 0.0 copy-start.5
  4.7 0.7 %copy-done.5 = f32[2]{0:T(128)S(1)} copy-done((f32[2]{0:T(128)S(1)}, f32[2]{0:T(128)}, u32[]{:S(2)}) %copy-start.5) | copy-done | bytes 32
  5.3 53.4 %shard_map.64 = f32[1,16,2,128,128]{4,3,2,1,0:T(8,128)S(1)} custom-call(f32[1,16,2,128,128]{4,3,2,1,0:T(8,128)S(1)} %copy-done, f32[128,128]{1,0:T(8,128)S(1)} %copy-done.2, f32[2,128,128]{2,1,0:T(8,128)S(1)} %copy-done.1, f32[2]{0:T(128)S(1)} %copy-done.3, f32[2]{0:T(128)S(1)} %copy-done.4, f32[2]{0:T(128)S(1)} %copy-done.5), custom_call_target="tpu_custom_call" | custom-call | tf_op jit(solution)/shard_map/pallas_call | solution.py:381
  58.7 1.3 %copy.8 = f32[1,16,2,128,128]{4,3,2,1,0:T(8,128)} copy(f32[1,16,2,128,128]{4,3,2,1,0:T(8,128)S(1)} %shard_map.64) | data formatting | bytes 4194304
Async XLA Ops:
  0.0 1.6 %copy-start = (f32[1,16,2,128,128]{4,3,2,1,0:T(8,128)S(1)}, f32[1,16,2,128,128]{4,3,2,1,0:T(8,128)}, u32[]{:S(2)}) copy-start(f32[1,16,2,128,128]{4,3,2,1,0:T(8,128)} %hier_ref.1) | copy-start | bytes 6291460
  1.6 0.9 %copy-start.1 = (f32[2,128,128]{2,1,0:T(8,128)S(1)}, f32[2,128,128]{2,1,0:T(8,128)}, u32[]{:S(2)}) copy-start(f32[2,128,128]{2,1,0:T(8,128)} %coup_ref.1) | copy-start | bytes 393220
  2.5 0.8 %copy-start.2 = (f32[128,128]{1,0:T(8,128)S(1)}, f32[128,128]{1,0:T(8,128)}, u32[]{:S(2)}) copy-start(f32[128,128]{1,0:T(8,128)} %ham_ref.1) | copy-start | bytes 196612
  3.3 0.7 %copy-start.3 = (f32[2]{0:T(128)S(1)}, f32[2]{0:T(128)}, u32[]{:S(2)}) copy-start(f32[2]{0:T(128)} %damp_ref.1) | copy-start | bytes 28
  4.0 0.7 %copy-start.4 = (f32[2]{0:T(128)S(1)}, f32[2]{0:T(128)}, u32[]{:S(2)}) copy-start(f32[2]{0:T(128)} %creal_ref.1) | copy-start | bytes 28
  4.6 0.7 %copy-start.5 = (f32[2]{0:T(128)S(1)}, f32[2]{0:T(128)}, u32[]{:S(2)}) copy-start(f32[2]{0:T(128)} %cimag_ref.1) | copy-start | bytes 28

commit v3 on v2

--- a/solution.py
+++ b/solution.py
@@ -23,9 +23,9 @@
     hier_ref,
     ham_ref,
     coup_ref,
-    damp_ref,
-    creal_ref,
-    cimag_ref,
+    damp_in,
+    creal_in,
+    cimag_in,
     out_ref,
     rho,
     mid,
@@ -36,9 +36,13 @@
     table,
     out_buf,
     ham_buf,
+    damp_ref,
+    creal_ref,
+    cimag_ref,
     own_sem,
     out_sem,
     ham_sem,
+    small_sem,
     send_sem,
     recv_sem,
 ):
@@ -166,7 +170,14 @@
         def _():
             partner_copy(i).start()
 
+    small = [
+        pltpu.make_async_copy(source, target, small_sem.at[k])
+        for k, (source, target) in enumerate(
+            ((damp_in, damp_ref), (creal_in, creal_ref), (cimag_in, cimag_ref))
+        )
+    ]
     for k in range(3):
+        small[k].start()
         operator_copy(k).start()
 
     @pl.loop(0, K)
@@ -183,6 +194,9 @@
             w_left[M : 2 * M, cols] = low
             w_right[cols, 0:M] = high
             w_right[cols, M : 2 * M] = low
+
+    for copy in small:
+        copy.wait()
 
     for mode in range(2):
         re = jnp.full((8, M), creal_ref[mode], jnp.float32)
@@ -377,11 +391,10 @@
     total = hierarchy.shape[1]
     M = hierarchy.shape[-1]
     hbm = pl.BlockSpec(memory_space=pltpu.HBM)
-    smem = pl.BlockSpec(memory_space=pltpu.SMEM)
     return pl.pallas_call(
         functools.partial(kernel, total, M),
         out_shape=jax.ShapeDtypeStruct(hierarchy.shape, jnp.float32),
-        in_specs=[hbm] * 3 + [smem] * 3,
+        in_specs=[hbm] * 6,
         out_specs=pl.BlockSpec(memory_space=pl.ANY),
         scratch_shapes=[
             pltpu.VMEM((4, total, 2, M, M), jnp.float32),
@@ -393,8 +406,12 @@
             pltpu.VMEM((6, total, 8, M), jnp.float32),
             pltpu.VMEM((total, 2, M, M), jnp.float32),
             pltpu.VMEM((3, M, M), jnp.float32),
+            pltpu.SMEM(damp_rates.shape, jnp.float32),
+            pltpu.SMEM(coef_real.shape, jnp.float32),
+            pltpu.SMEM(coef_imag.shape, jnp.float32),
             pltpu.SemaphoreType.DMA((total,)),
             pltpu.SemaphoreType.DMA((total,)),
+            pltpu.SemaphoreType.DMA((3,)),
             pltpu.SemaphoreType.DMA((3,)),
             pltpu.SemaphoreType.DMA((5, total)),
             pltpu.SemaphoreType.DMA((4, total)),
@@ -402,7 +419,19 @@
         compiler_params=pltpu.CompilerParams(
             collective_id=0, has_side_effects=True, vmem_limit_bytes=(8 + total) * 2**20
         ),
-    )(hierarchy, hamiltonian, couplings, damp_rates, coef_real, coef_imag)
+    )(
+        *(
+            pltpu.with_memory_space_constraint(x, pltpu.HBM)
+            for x in (
+                hierarchy,
+                hamiltonian,
+                couplings,
+                damp_rates,
+                coef_real,
+                coef_imag,
+            )
+        )
+    )
 
 
 def solution(mesh):

time: 60.2 us -> 54.5 us (0.905)
  the two profiles are of different devices: /device:TPU:4 before, /device:TPU:6 now
where the time goes in v3:
time: 54.5 us; the launch traced here: 54.3 us
  Pallas kernels  53 us (97%)
  local copies, waits for them, and re-layouts  1.32 us (2%)
    pallas_call x1, Pallas kernels, per_device(): pl.pallas_call(functools.partial(kernel, total, M), out_shape=jax.ShapeDt...  53 us
    unnamed x1, local copies, waits for them, and re-layouts  1.32 us

profile of v3, /device:TPU:6, one launch (start us, length us, event | category | flops | bytes accessed | tf_op | source)
XLA Modules:
  0.0 54.3 jit_solution(16737256207412074501)
XLA Ops:
  0.0 53.0 %shard_map.64 = f32[1,16,2,128,128]{4,3,2,1,0:T(8,128)S(1)} custom-call(f32[1,16,2,128,128]{4,3,2,1,0:T(8,128)} %hier_ref.1, f32[128,128]{1,0:T(8,128)} %ham_ref.1, f32[2,128,128]{2,1,0:T(8,128)} %coup_ref.1, f32[2]{0:T(128)} %damp_in.1, f32[2]{0:T(128)} %creal_in.1, f32[2]{0:T(128)} %cimag_in.1), custom_call_target="tpu_custom_call" | custom-call | tf_op jit(solution)/shard_map/pallas_call | solution.py:394
  53.0 1.3 %copy.8 = f32[1,16,2,128,128]{4,3,2,1,0:T(8,128)} copy(f32[1,16,2,128,128]{4,3,2,1,0:T(8,128)S(1)} %shard_map.64) | data formatting | bytes 4194304

commit v4 on v3

--- a/solution.py
+++ b/solution.py
@@ -10,6 +10,7 @@
 MESH = pl.DeviceIdType.MESH
 NEAR, OWN, PARTNER, FAR = 0, 1, 2, 3
 STRIP = 32
+LAG = 2
 
 
 def split(x):
@@ -322,8 +323,28 @@
     def _(i):
         out_copy(i).start()
 
-    @pl.loop(-1, K)
-    def _(i):
+    @pl.loop(-1, K + LAG)
+    def _(i):
+        j = i - LAG
+
+        @pl.when(j >= 1)
+        def _():
+            out_copy(j - 1).start()
+
+        @pl.when(j >= 0)
+        def _():
+            @pl.when(j < pairs)
+            def _():
+                mid_copy(j).wait_recv()
+
+            def store(part, value):
+                out_buf[j, part] = value
+
+            derivative(
+                mid, OWN, up, down, p, j,
+                lambda part: rho[OWN, j, part], step_size, store,
+            )
+
         take_own(i + 2)
         take(i + 1)
 
@@ -342,26 +363,6 @@
         @pl.when(i + 1 < pairs)
         def _():
             mid_copy(i + 1).start()
-
-        @pl.when(i >= 1)
-        def _():
-            out_copy(i - 1).start()
-
-        @pl.when(i >= 0)
-        def _():
-            @pl.when(i < pairs)
-            def _():
-                mid_copy(i).wait_recv()
-
-            def store(part, value):
-                out_buf[i, part] = value
-
-            derivative(
-                mid, OWN, up, down, p, i,
-                lambda part: rho[OWN, i, part], step_size, store,
-            )
-
-    take(K + 1)
 
     out_copy(K - 1).start()
 

time: 54.5 us -> 51.6 us (0.947)
  the two profiles are of different devices: /device:TPU:6 before, /device:TPU:0 now
where the time goes in v4:
time: 51.6 us; the launch traced here: 51.5 us
  Pallas kernels  50.2 us (97%)
  local copies, waits for them, and re-layouts  1.32 us (3%)
    pallas_call x1, Pallas kernels, per_device(): pl.pallas_call(functools.partial(kernel, total, M), out_shape=jax.ShapeDt...  50.2 us
    unnamed x1, local copies, waits for them, and re-layouts  1.32 us

profile of v4, /device:TPU:0, one launch (start us, length us, event | category | flops | bytes accessed | tf_op | source)
XLA Modules:
  0.0 51.5 jit_solution(17873319563937658086)
XLA Ops:
  0.0 50.2 %shard_map.64 = f32[1,16,2,128,128]{4,3,2,1,0:T(8,128)S(1)} custom-call(f32[1,16,2,128,128]{4,3,2,1,0:T(8,128)} %hier_ref.1, f32[128,128]{1,0:T(8,128)} %ham_ref.1, f32[2,128,128]{2,1,0:T(8,128)} %coup_ref.1, f32[2]{0:T(128)} %damp_in.1, f32[2]{0:T(128)} %creal_in.1, f32[2]{0:T(128)} %cimag_in.1), custom_call_target="tpu_custom_call" | custom-call | tf_op jit(solution)/shard_map/pallas_call | solution.py:395
  50.2 1.3 %copy.8 = f32[1,16,2,128,128]{4,3,2,1,0:T(8,128)} copy(f32[1,16,2,128,128]{4,3,2,1,0:T(8,128)S(1)} %shard_map.64) | data formatting | bytes 4194304

commit v5 on v4

--- a/solution.py
+++ b/solution.py
@@ -11,6 +11,7 @@
 NEAR, OWN, PARTNER, FAR = 0, 1, 2, 3
 STRIP = 32
 LAG = 2
+EARLY = 3
 
 
 def split(x):
@@ -286,11 +287,6 @@
     near_down = jnp.where(first, FAR, OWN)
     near_q = jnp.where(first, p - 1, p + 1)
 
-    def take_own(i):
-        @pl.when(i < K)
-        def _():
-            own_copy(i).wait()
-
     def take(i):
         @pl.when(i < near_count)
         def _():
@@ -317,7 +313,13 @@
             lambda part: rho[which, i, part], 0.5 * step_size, store,
         )
 
-    take_own(jnp.int32(0))
+    early = jnp.logical_and(core == 1, K - 1 > EARLY + 1)
+    in_turn = jnp.where(early, K - 1, K)
+
+    @pl.loop(0, K)
+    def _(i):
+        own_copy(i).wait()
+
 
     @pl.loop(K, N)
     def _(i):
@@ -345,24 +347,37 @@
                 lambda part: rho[OWN, j, part], step_size, store,
             )
 
-        take_own(i + 2)
         take(i + 1)
 
-        @pl.when(i + 1 < pairs)
+        @pl.when(jnp.logical_and(i < EARLY, i + 1 < pairs))
         def _():
             arrival(PARTNER, i + 1).wait_recv()
 
-        @pl.when(i + 1 < K)
+        @pl.when(i == EARLY)
+        def _():
+            @pl.loop(EARLY + 1, pairs)
+            def _(k):
+                arrival(PARTNER, k).wait_recv()
+
+        @pl.when(i + 1 < in_turn)
         def _():
             middle(OWN, i + 1, up, down, p)
 
+        @pl.when(jnp.logical_and(early, i == EARLY))
+        def _():
+            middle(OWN, K - 1, up, down, p)
+
         @pl.when(jnp.logical_and(i >= 0, i < mid_near_count))
         def _():
             middle(NEAR, i, near_up, near_down, near_q)
 
-        @pl.when(i + 1 < pairs)
+        @pl.when(jnp.logical_and(i + 1 < pairs, i + 1 < in_turn))
         def _():
             mid_copy(i + 1).start()
+
+        @pl.when(jnp.logical_and(early, i == EARLY))
+        def _():
+            mid_copy(K - 1).start()
 
     out_copy(K - 1).start()
 

time: 51.6 us -> 50.9 us (0.986)
  Pallas kernels: 50.2 us -> 49.4 us
    pallas_call x1, Pallas kernels: 50.2 us -> 49.4 us  [per_device(): pl.pallas_call(functools.partial(kernel, total, M), out_shape=jax.ShapeDt...]
where the time goes in v5:
time: 50.9 us; the launch traced here: 50.7 us
  Pallas kernels  49.4 us (97%)
  local copies, waits for them, and re-layouts  1.32 us (3%)
    pallas_call x1, Pallas kernels, per_device(): pl.pallas_call(functools.partial(kernel, total, M), out_shape=jax.ShapeDt...  49.4 us
    unnamed x1, local copies, waits for them, and re-layouts  1.32 us

profile of v5, /device:TPU:0, one launch (start us, length us, event | category | flops | bytes accessed | tf_op | source)
XLA Modules:
  0.0 50.7 jit_solution(8646163740102811541)
XLA Ops:
  0.0 49.4 %shard_map.64 = f32[1,16,2,128,128]{4,3,2,1,0:T(8,128)S(1)} custom-call(f32[1,16,2,128,128]{4,3,2,1,0:T(8,128)} %hier_ref.1, f32[128,128]{1,0:T(8,128)} %ham_ref.1, f32[2,128,128]{2,1,0:T(8,128)} %coup_ref.1, f32[2]{0:T(128)} %damp_in.1, f32[2]{0:T(128)} %creal_in.1, f32[2]{0:T(128)} %cimag_in.1), custom_call_target="tpu_custom_call" | custom-call | tf_op jit(solution)/shard_map/pallas_call | solution.py:410
  49.4 1.3 %copy.8 = f32[1,16,2,128,128]{4,3,2,1,0:T(8,128)} copy(f32[1,16,2,128,128]{4,3,2,1,0:T(8,128)S(1)} %shard_map.64) | data formatting | bytes 4194304

commit v6 on v5

--- a/solution.py
+++ b/solution.py
@@ -325,9 +325,11 @@
     def _(i):
         out_copy(i).start()
 
-    @pl.loop(-1, K + LAG)
-    def _(i):
-        j = i - LAG
+    lag = jnp.where(p == 1, 1, LAG)
+
+    @pl.loop(-1, K + lag)
+    def _(i):
+        j = i - lag
 
         @pl.when(j >= 1)
         def _():

time: 50.9 us -> 50.8 us (level)
  no operation moved by 1% of the time
where the time goes in v6:
time: 50.8 us; the launch traced here: 50.7 us
  Pallas kernels  49.4 us (97%)
  local copies, waits for them, and re-layouts  1.32 us (3%)
    pallas_call x1, Pallas kernels, per_device(): pl.pallas_call(functools.partial(kernel, total, M), out_shape=jax.ShapeDt...  49.4 us
    unnamed x1, local copies, waits for them, and re-layouts  1.32 us

profile of v6, /device:TPU:0, one launch (start us, length us, event | category | flops | bytes accessed | tf_op | source)
XLA Modules:
  0.0 50.7 jit_solution(5803903192229317566)
XLA Ops:
  0.0 49.4 %shard_map.64 = f32[1,16,2,128,128]{4,3,2,1,0:T(8,128)S(1)} custom-call(f32[1,16,2,128,128]{4,3,2,1,0:T(8,128)} %hier_ref.1, f32[128,128]{1,0:T(8,128)} %ham_ref.1, f32[2,128,128]{2,1,0:T(8,128)} %coup_ref.1, f32[2]{0:T(128)} %damp_in.1, f32[2]{0:T(128)} %creal_in.1, f32[2]{0:T(128)} %cimag_in.1), custom_call_target="tpu_custom_call" | custom-call | tf_op jit(solution)/shard_map/pallas_call | solution.py:412
  49.4 1.3 %copy.8 = f32[1,16,2,128,128]{4,3,2,1,0:T(8,128)} copy(f32[1,16,2,128,128]{4,3,2,1,0:T(8,128)S(1)} %shard_map.64) | data formatting | bytes 4194304
